TPU v7x, 32 devices: a whole 2x2x4 slice. The times are simulated.
32 devices in a mesh: groups: 2 (over y), seq: 4 (over z), rows: 2 (over x), cfg: 2 (over core).
Axes of the slice: x: 2, y: 2, z: 4, core: 2. Of those that a mesh axis runs over, the one named last changes fastest.
Arguments:
- hidden: bfloat16 [2, 4096, 5120], P('cfg', ('groups', 'seq', 'rows')), parts along dimension 1, may hold values from -500 to 500
- token_order: int32 [4096], P(('groups', 'seq', 'rows')), parts along dimension 0, may hold values from 0 to 2047, as said below
- noisy_latent: float32 [16, 8, 2048], P(('groups', 'seq'), ('rows', 'cfg')), parts along dimension 0, may hold values from -6 to 6
- head_weight: bfloat16 [5120, 64], replicated, may hold values from -0.078125 to 0.078125
- head_mod: float32 [2, 5120], replicated, may hold values from -2.5 to 2.5
- guidance: float32 [1], replicated, may hold values from 3 to 7
- timestep_index: int32 [1], replicated, may hold values from 0 to 7
- step_table: int32 [9], replicated, may hold values from 0 to 1000, as said below
- vae_mean: float32 [16], replicated, may hold values from -2.5 to 2.5
- vae_std: float32 [16], replicated, may hold values from 1.1 to 3.3
- conv2_weight: float32 [16, 16], replicated, may hold values from -1.5 to 1.5
- conv2_bias: float32 [16], replicated, may hold values from -2.5 to 2.5
- conv1_weight: bfloat16 [27, 16, 384], replicated, may hold values from -0.3125 to 0.3125
- conv1_bias: float32 [384], replicated, may hold values from -2.5 to 2.5
Outputs:
- decoded: bfloat16 [16, 8, 128, 384], P(('groups', 'seq'), ('rows', 'cfg')), parts along dimension 0
There are 2 independent parts, one for each index of `groups`. A program takes and returns all parts, laid end to end along the dimension named above; an argument that names none is the same for every part. Nothing has to cross between parts.
Inputs may be any that keep to these rules, and one draw needn't show every extreme that they name: `token_order`: a permutation of the 2048 cells, cell f * 4 * 64 + i * 64 + j being token column j of token row i of frame f; positions k * 256 to (k + 1) * 256 - 1 with k = s * 2 + r hold exactly the cells of frames s * 2 to (s + 1) * 2 - 1 and token rows r * 2 to (r + 1) * 2 - 1. `step_table`: strictly decreasing from 1000 to 0; consecutive entries differ by 90 or more.
All inputs are finite; a program needn't handle non-finite values.
Results may differ from a plain program's by a relative error of at most 0.0053.
Values may be sent and summed in bfloat16 or wider, within the bound.
No kernel may reach another device: no remote copies, remote signals or barrier semaphores. Data moves between devices by JAX's collectives and lax.ppermute only.
A program may use at most 64 MiB of HBM per device.

v0:
```python
import jax
import jax.numpy as jnp
from jax import lax
from jax.sharding import PartitionSpec as P

FR_DEV = 2
TR_DEV = 2
WT = 64


def padded_2(block, sides, width):
    for axis, dim in sides:
        count = lax.axis_size(axis)
        forward = [(i, i + 1) for i in range(count - 1)]
        backward = [(target, source) for source, target in forward]
        low = lax.ppermute(
            lax.slice_in_dim(block, block.shape[dim] - width, None, axis=dim), axis, forward
        )
        high = lax.ppermute(lax.slice_in_dim(block, 0, width, axis=dim), axis, backward)
        block = jnp.concatenate([low, block, high], axis=dim)
    return block


def shifted(block, axis, distance):
    devices = range(lax.axis_size(axis))
    route = [(i - distance, i) for i in devices if i - distance in devices]
    return lax.ppermute(block, axis, route)


def head_rows(row_block, head_weight, head_mod):
    values = row_block.astype(jnp.float32)
    center = jnp.mean(values, axis=-1, keepdims=True)
    spread = jnp.mean(jnp.square(values - center), axis=-1, keepdims=True)
    normed = (values - center) * lax.rsqrt(spread + 1e-06)
    head_in = (normed * (1.0 + head_mod[1]) + head_mod[0]).astype(jnp.bfloat16)
    return jnp.dot(head_in, head_weight, preferred_element_type=jnp.float32)


def conv_taps(padded, frames, row_count, col_count):
    pieces = []
    for step_time in range(3):
        for step_row in range(3):
            for step_col in range(3):
                pieces.append(
                    padded[
                        step_time : step_time + frames,
                        step_row : step_row + row_count,
                        step_col : step_col + col_count,
                        :,
                    ]
                )
    return jnp.concatenate(pieces, axis=-1)


def per_device(
    hidden,
    token_order,
    noisy_latent,
    head_weight,
    head_mod,
    guidance,
    timestep_index,
    step_table,
    vae_mean,
    vae_std,
    conv2_weight,
    conv2_bias,
    conv1_weight,
    conv1_bias,
):
    token_count = hidden.shape[1]
    patch_width = head_weight.shape[1]
    lat_channels = vae_mean.shape[0]
    out_channels = conv1_weight.shape[2]
    token_rows = TR_DEV * lax.axis_size("rows")
    own_head = head_rows(hidden[0], head_weight, head_mod)
    frame_pos = token_order // (token_rows * WT) % FR_DEV
    row_pos = token_order // WT % TR_DEV
    col_pos = token_order % WT
    local_cell = (frame_pos * TR_DEV + row_pos) * WT + col_pos
    placed = jnp.zeros((token_count, patch_width), jnp.float32).at[local_cell].set(own_head)
    local_block = placed.reshape(FR_DEV, TR_DEV, WT, 2, 2, lat_channels).transpose(0, 1, 3, 2, 4, 5)
    local_block = local_block.reshape(FR_DEV, 2, TR_DEV, 2 * WT * lat_channels)
    gathered = lax.all_gather(local_block[None], "cfg", axis=0, tiled=True)
    half_index = lax.axis_index("cfg")
    conditional = lax.dynamic_index_in_dim(gathered[0], half_index, 1, keepdims=False)
    unconditional = lax.dynamic_index_in_dim(gathered[1], half_index, 1, keepdims=False)
    velocity = unconditional + guidance[0] * (conditional - unconditional)
    step_index = timestep_index[0]
    sigma_now = step_table[step_index].astype(jnp.float32) / 1000.0
    sigma_next = step_table[step_index + 1].astype(jnp.float32) / 1000.0
    stepped = noisy_latent + (sigma_next - sigma_now) * velocity
    channels = stepped.reshape(FR_DEV, TR_DEV, 2 * WT, lat_channels) * vae_std + vae_mean
    mixed_lat = (
        jnp.einsum("fyxc,cd->fyxd", channels, conv2_weight, precision=lax.Precision.HIGHEST)
        + conv2_bias
    )
    latent_in = mixed_lat.astype(jnp.bfloat16).reshape(FR_DEV, TR_DEV, 2 * WT * lat_channels)
    framed = padded_2(latent_in, ((("rows", "cfg"), 1),), 1)
    earlier = shifted(framed, "seq", 1)
    padded = jnp.concatenate([earlier, framed], axis=0).reshape(
        FR_DEV + 2, TR_DEV + 2, 2 * WT, lat_channels
    )
    padded = jnp.pad(padded, ((0, 0), (0, 0), (1, 1), (0, 0)))
    tap_columns = conv_taps(padded, FR_DEV, TR_DEV, 2 * WT).reshape(
        FR_DEV * TR_DEV * 2 * WT, 27 * lat_channels
    )
    kernel = conv1_weight.reshape(27 * lat_channels, out_channels)
    result = jnp.dot(tap_columns, kernel, preferred_element_type=jnp.float32) + conv1_bias
    return result.astype(jnp.bfloat16).reshape(FR_DEV, TR_DEV, 2 * WT, out_channels)


def solution(mesh):
    return jax.shard_map(
        per_device,
        mesh=mesh,
        in_specs=(
            P("cfg", ("groups", "seq", "rows"), None),
            P(("groups", "seq", "rows")),
            P(("groups", "seq"), ("rows", "cfg"), None),
            P(),
            P(),
            P(),
            P(),
            P(),
            P(),
            P(),
            P(),
            P(),
            P(),
            P(),
        ),
        out_specs=P(("groups", "seq"), ("rows", "cfg"), None, None),
        check_vma=False,
    )
```

profile of v0, /device:TPU:1, one launch (start us, length us, event | category | flops | bytes accessed | tf_op | source)
XLA Modules:
  0.0 36.1 jit_solution(17837188760740041675)
XLA Ops:
  0.8 1.4 %fusion.30 = (s32[1]{0:T(128)}, s32[1]{0:T(128)}) fusion(s32[9]{0:T(128)} %param.21, s32[]{:T(128)S(6)} %select_n.38, s32[]{:T(128)S(6)} %select_n.37), kind=kLoop, calls=%fused_computation.73 | loop fusion | bytes 24 | tf_op jit(solution)/shard_map/dynamic_slice | solution.py:90
  3.5 0.9 %slice_add_fusion = (f32[1,5120]{1,0:T(1,128)S(1)}, f32[1,5120]{1,0:T(1,128)S(1)}) fusion(f32[2,5120]{1,0:T(2,128)} %param.18), kind=kLoop, calls=%fused_computation.26 | loop fusion | flops 5120 | bytes 81920 | tf_op jit(solution)/shard_map/add | solution.py:35
  4.4 2.2 %convert_reduce_fusion = f32[256]{0:T(256)S(1)} fusion(bf16[1,256,5120]{2,1,0:T(8,128)(2,1)} %param.14), kind=kLoop, calls=%fused_computation.1 | loop fusion | flops 2621184 | bytes 2622464 | tf_op jit(solution)/shard_map/reduce_sum | solution.py:32
  6.6 0.8 %fusion.3 = f32[256]{0:T(256)S(1)} fusion(bf16[1,256,5120]{2,1,0:T(8,128)(2,1)S(1)} %copy-done.1, f32[256]{0:T(256)S(1)} %broadcast_multiply_fusion), kind=kLoop, calls=%fused_computation.6 | loop fusion | flops 5242624 | bytes 2623488 | tf_op jit(solution)/shard_map/reduce_sum | solution.py:33
  7.5 1.1 %fusion.7 = f32[256,64]{1,0:T(8,128)S(1)} fusion(bf16[5120,64]{0,1:T(8,128)(2,1)S(1)} %copy-done, bf16[1,256,5120]{2,1,0:T(8,128)(2,1)S(1)} %copy-done.1, f32[5120]{0:T(1024)S(1)} %bitcast.57, f32[5120]{0:T(1024)S(1)} %bitcast.56, f32[256]{0:T(256)S(1)} %add_rsqrt_fusion, f32[256]{0:T(256)S(1)} %broadcast_multiply_fusion), kind=kOutput, calls=%fused_computation.10 | convolution fusion | flops 175636480 | bytes 3385344 | tf_op jit(solution)/shard_map/dot_general | solution.py:36
  8.7 0.0 copy-start.6
  8.7 0.0 copy-start.7
  8.7 1.2 %scatter_custom_fusion = f32[256,64]{1,0:T(8,128)S(1)} fusion(s32[256]{0:T(256)S(1)} %compare_select_fusion, f32[256,64]{1,0:T(8,128)S(1)} %fusion.7, f32[]{:T(128)} %constant.82.clone.1), kind=kCustom, calls=%fused_computation.16 | custom fusion | bytes 65540 | tf_op jit(solution)/shard_map/scatter | solution.py:81
  9.9 0.1 copy.30
  10.0 0.1 reshape.49
  10.1 0.3 copy.31
  10.4 0.7 %broadcast_in_dim_reshape.3 = f32[1,2,2,2,2048]{4,3,2,1,0:T(2,128)S(1)} reshape(f32[2,2,2,64,2,16]{5,4,3,2,1,0:T(2,128)S(1)} %copy.31) | data formatting | bytes 131072 | tf_op jit(solution)/shard_map/broadcast_in_dim;reshape | solution.py:84
  11.1 1.9 %all_gather.3 = f32[2,2,2,2,2048]{4,3,2,1,0:T(2,128)S(1)} all-gather(f32[1,2,2,2,2048]{4,3,2,1,0:T(2,128)S(1)} %broadcast_in_dim_reshape.3), channel_id=1, replica_groups=mesh['groups'=2,'seq'=4,'rows'=2,'cfg'=2] {'cfg'}, dimensions={0}, use_global_device_ids=true | all-gather | bytes 196608 | tf_op jit(solution)/shard_map/all_gather | solution.py:84
  13.7 0.1 reshape.50
  13.8 0.1 copy.32
  13.9 0.0 copy-done.7
  14.0 0.2 fusion.10
  14.2 0.1 copy.34
  14.3 0.2 reshape.51
  14.5 4.5 %collective-permute-start = (bf16[2,1,2048]{2,1,0:T(2,128)(2,1)S(1)}, bf16[2,1,2048]{2,1,0:T(2,128)(2,1)S(1)}, u32[]{:S(2)}, u32[]{:S(2)}) collective-permute-start(bf16[2,1,2048]{2,1,0:T(2,128)(2,1)S(1)} %get-tuple-element.36), channel_id=1, source_target_pairs={{0,1},{1,2},{2,3},{4,5},{5,6},{6,7},{8,9},{9,10},{10,11},{12,13},{... | collective-permute-start | bytes 24584 | tf_op jit(solution)/shard_map/ppermute | solution.py:16
  19.0 1.9 %collective-permute-start.1 = (bf16[2,1,2048]{2,1,0:T(2,128)(2,1)S(1)}, bf16[2,1,2048]{2,1,0:T(2,128)(2,1)S(1)}, u32[]{:S(2)}, u32[]{:S(2)}) collective-permute-start(bf16[2,1,2048]{2,1,0:T(2,128)(2,1)S(1)} %get-tuple-element.37), channel_id=1, source_target_pairs={{1,0},{2,1},{3,2},{5,4},{6,5},{7,6},{9,8},{10,9},{11,10},{13,12},{... | collective-permute-start | bytes 24584 | tf_op jit(solution)/shard_map/ppermute | solution.py:19
  21.0 3.1 %collective-permute-done.1 = bf16[2,1,2048]{2,1,0:T(2,128)(2,1)S(1)} collective-permute-done((bf16[2,1,2048]{2,1,0:T(2,128)(2,1)S(1)}, bf16[2,1,2048]{2,1,0:T(2,128)(2,1)S(1)}, u32[]{:S(2)}, u32[]{:S(2)}) %collective-permute-start.1) | collective-permute-done | bytes 8224 | tf_op jit(solution)/shard_map/ppermute | solution.py:19
  24.1 0.1 pad_maximum_fusion
  24.2 3.2 %collective-permute-start.2 = (bf16[2,4,2048]{2,1,0:T(4,128)(2,1)S(1)}, bf16[2,4,2048]{2,1,0:T(4,128)(2,1)S(1)}, u32[]{:S(2)}, u32[]{:S(2)}) collective-permute-start(bf16[2,4,2048]{2,1,0:T(4,128)(2,1)S(1)} %pad_maximum_fusion), channel_id=1, source_target_pairs={{0,4},{4,8},{8,12},{1,5},{5,9},{9,13},{2,6},{6,10},{10,14},{3,7},{... | collective-permute-start | bytes 98312 | tf_op jit(solution)/shard_map/ppermute | solution.py:27
  27.4 1.0 %collective-permute-done.2 = bf16[2,4,2048]{2,1,0:T(4,128)(2,1)S(1)} collective-permute-done((bf16[2,4,2048]{2,1,0:T(4,128)(2,1)S(1)}, bf16[2,4,2048]{2,1,0:T(4,128)(2,1)S(1)}, u32[]{:S(2)}, u32[]{:S(2)}) %collective-permute-start.2) | collective-permute-done | bytes 32800 | tf_op jit(solution)/shard_map/ppermute | solution.py:27
  28.4 0.1 maximum_maximum_fusion
  28.5 0.4 %reshape.52 = bf16[4,4,128,16]{3,2,1,0:T(8,128)(2,1)S(1)} reshape(bf16[4,4,2048]{2,1,0:T(4,128)(2,1)S(1)} %maximum_maximum_fusion) | data formatting | bytes 131072 | tf_op jit(solution)/shard_map/reshape | solution.py:101
  28.8 0.3 pad_slice_fusion.1
  29.1 1.0 %pad_slice_fusion = (bf16[2,2,128,16]{3,2,1,0:T(8,128)(2,1)S(1)}, bf16[2,2,128,16]{3,2,1,0:T(8,128)(2,1)S(1)}, bf16[2,2,128,16]{3,2,1,0:T(8,128)(2,1)S(1)}, bf16...) fusion(bf16[4,4,128,16]{3,2,1,0:T(8,128)(2,1)S(1)} %reshape.52), kind=kLoop, calls=%fused_computation.52 | loop fusion | bytes 819200 | tf_op jit(solution)/shard_map/slice | solution.py:45
  30.1 0.9 %fusion.27 = (bf16[2,2,128,16]{3,2,1,0:T(8,128)(2,1)}, bf16[2,2,128,16]{3,2,1,0:T(8,128)(2,1)}, bf16[2,2,128,16]{3,2,1,0:T(8,128)(2,1)}, bf16[2,2,128,16]{3,2,1,...) fusion(bf16[4,4,128,16]{3,2,1,0:T(8,128)(2,1)S(1)} %reshape.52), kind=kLoop, calls=%fused_computation.70 | loop fusion | bytes 1277952 | tf_op jit(solution)/shard_map/slice | solution.py:45
  31.0 2.9 %concatenate.11 = bf16[2,2,128,432]{3,2,1,0:T(8,128)(2,1)S(1)} concatenate(bf16[2,2,128,16]{3,2,1,0:T(8,128)(2,1)} %get-tuple-element.31, bf16[2,2,128,16]{3,2,1,0:T(8,128)(2,1)} %get-tuple-element.30, bf16[2,2,128,16]{3,2,1,0:T(8,128)(2,1)S(1)} %get-tuple-element.6, bf16[2,2,128,16]{3,2,1,0:T(8,128)(2,1)S(1)} %get-tuple-element.7, bf16[2,2,128,16]{3,2,1,0:T(8,128)(2,1)} %get-tuple-element.29, ...), dimensions={3} | concatenate | bytes 884736 | tf_op jit(solution)/shard_map/concatenate | solution.py:52
  33.9 2.2 %fusion.9 = bf16[512,384]{1,0:T(8,128)(2,1)} fusion(bf16[512,432]{1,0:T(8,128)(2,1)S(1)} %bitcast.55, bf16[432,384]{1,0:T(8,128)(2,1)} %bitcast.58, f32[384]{0:T(512)S(1)} %copy-done.5), kind=kOutput, calls=%fused_computation.12 | convolution fusion | flops 170262528 | bytes 1168896 | tf_op jit(solution)/shard_map/dot_general | solution.py:109
  (22 shorter events, 0.2 us)
Async XLA Ops:
  0.0 7.5 %copy-start = (bf16[5120,64]{0,1:T(8,128)(2,1)S(1)}, bf16[5120,64]{0,1:T(8,128)(2,1)}, u32[]{:S(2)}) copy-start(bf16[5120,64]{0,1:T(8,128)(2,1)} %param.17) | copy-start | bytes 1966084
  0.0 6.6 %copy-start.1 = (bf16[1,256,5120]{2,1,0:T(8,128)(2,1)S(1)}, bf16[1,256,5120]{2,1,0:T(8,128)(2,1)}, u32[]{:S(2)}) copy-start(bf16[1,256,5120]{2,1,0:T(8,128)(2,1)} %param.14) | copy-start | bytes 7864324
  4.4 3.0 %copy-start.3 = (s32[256]{0:T(256)S(1)}, s32[256]{0:T(256)}, u32[]{:S(2)}) copy-start(s32[256]{0:T(256)} %param.15) | copy-start | bytes 3076
  7.5 6.2 %copy-start.2 = (f32[2,2,2048]{2,1,0:T(2,128)S(1)}, f32[2,2,2048]{2,1,0:T(2,128)}, u32[]{:S(2)}) copy-start(f32[2,2,2048]{2,1,0:T(2,128)} %param.16) | copy-start | bytes 98308
  8.6 5.3 %copy-start.4 = (f32[16,16]{1,0:T(8,128)S(1)}, f32[16,16]{1,0:T(8,128)}, u32[]{:S(2)}) copy-start(f32[16,16]{1,0:T(8,128)} %param.24) | copy-start | bytes 3076
  8.7 5.3 %copy-start.6 = (f32[16]{0:T(128)S(1)}, f32[16]{0:T(128)}, u32[]{:S(2)}) copy-start(f32[16]{0:T(128)} %param.25) | copy-start | bytes 196
  8.7 5.3 %copy-start.7 = (f32[16]{0:T(128)S(1)}, f32[16]{0:T(128)}, u32[]{:S(2)}) copy-start(f32[16]{0:T(128)} %param.22) | copy-start | bytes 196
  8.7 5.3 %copy-start.8 = (f32[16]{0:T(128)S(1)}, f32[16]{0:T(128)}, u32[]{:S(2)}) copy-start(f32[16]{0:T(128)} %param.23) | copy-start | bytes 196
  14.5 6.4 %collective-permute-start = (bf16[2,1,2048]{2,1,0:T(2,128)(2,1)S(1)}, bf16[2,1,2048]{2,1,0:T(2,128)(2,1)S(1)}, u32[]{:S(2)}, u32[]{:S(2)}) collective-permute-start(bf16[2,1,2048]{2,1,0:T(2,128)(2,1)S(1)} %get-tuple-element.36), channel_id=1, source_target_pairs={{0,1},{1,2},{2,3},{4,5},{5,6},{6,7},{8,9},{9,10},{10,11},{12,13},{... | collective-permute-start | bytes 24584 | tf_op jit(solution)/shard_map/ppermute | solution.py:16
  19.0 5.1 %collective-permute-start.1 = (bf16[2,1,2048]{2,1,0:T(2,128)(2,1)S(1)}, bf16[2,1,2048]{2,1,0:T(2,128)(2,1)S(1)}, u32[]{:S(2)}, u32[]{:S(2)}) collective-permute-start(bf16[2,1,2048]{2,1,0:T(2,128)(2,1)S(1)} %get-tuple-element.37), channel_id=1, source_target_pairs={{1,0},{2,1},{3,2},{5,4},{6,5},{7,6},{9,8},{10,9},{11,10},{13,12},{... | collective-permute-start | bytes 24584 | tf_op jit(solution)/shard_map/ppermute | solution.py:19
  24.2 4.2 %collective-permute-start.2 = (bf16[2,4,2048]{2,1,0:T(4,128)(2,1)S(1)}, bf16[2,4,2048]{2,1,0:T(4,128)(2,1)S(1)}, u32[]{:S(2)}, u32[]{:S(2)}) collective-permute-start(bf16[2,4,2048]{2,1,0:T(4,128)(2,1)S(1)} %pad_maximum_fusion), channel_id=1, source_target_pairs={{0,4},{4,8},{8,12},{1,5},{5,9},{9,13},{2,6},{6,10},{10,14},{3,7},{... | collective-permute-start | bytes 98312 | tf_op jit(solution)/shard_map/ppermute | solution.py:27
  30.1 3.8 %copy-start.5 = (f32[384]{0:T(512)S(1)}, f32[384]{0:T(512)}, u32[]{:S(2)}) copy-start(f32[384]{0:T(512)} %param.27) | copy-start | bytes 4612
where the time goes:
time: 36.6 us; the launch traced here: 36.1 us
  local copies, waits for them, and re-layouts  9.76 us (27%)
  starting transfers between devices  9.62 us (26%)
  waiting for transfers between devices  4.13 us (11%)
  other arithmetic  4.12 us (11%)
  matrix products  3.55 us (10%)
  between operations  2.99 us (8%)
  blocking collectives  1.9 us (5%)
    ppermute x1, starting transfers between devices, padded_2(): lax.ppermute(lax.slice_in_dim(block, block.shape[dim] - width, None, axis...  4.5 us
    ppermute x1, starting transfers between devices, shifted(): return lax.ppermute(block, axis, route)  3.2 us
    ppermute x1, waiting for transfers between devices, padded_2(): lax.ppermute(lax.slice_in_dim(block, 0, width, axis=dim), axis, backward)  3.12 us
    concatenate x1, local copies, waits for them, and re-layouts, conv_taps(): return jnp.concatenate(pieces, axis=-1)  2.88 us
    reduce_sum x1, other arithmetic, head_rows(): center = jnp.mean(values, axis=-1, keepdims=True)  2.18 us
    slice x3, local copies, waits for them, and re-layouts, conv_taps(): padded[step_time:step_time + frames, step_row:step_row + row_count, step_...  2.17 us
    dot_general x1, matrix products, per_device(): jnp.dot(tap_columns, kernel, preferred_element_type=jnp.float32)  2.16 us
    ppermute x1, starting transfers between devices, padded_2(): lax.ppermute(lax.slice_in_dim(block, 0, width, axis=dim), axis, backward)  1.92 us
  transfers between devices with their start and end apart: 3, of which 2 were waited for; matrix products, arithmetic and copies ran while one was open for 0% of the time, Pallas kernels for 0%

commit v1 on v0

--- a/solution.py
+++ b/solution.py
@@ -81,7 +81,11 @@
     placed = jnp.zeros((token_count, patch_width), jnp.float32).at[local_cell].set(own_head)
     local_block = placed.reshape(FR_DEV, TR_DEV, WT, 2, 2, lat_channels).transpose(0, 1, 3, 2, 4, 5)
     local_block = local_block.reshape(FR_DEV, 2, TR_DEV, 2 * WT * lat_channels)
-    gathered = lax.all_gather(local_block[None], "cfg", axis=0, tiled=True)
+    x = local_block[None]
+    size = lax.axis_size("cfg")
+    blocks = jnp.stack([x for _ in range(size)])
+    blocks = lax.all_to_all(blocks, "cfg", split_axis=0, concat_axis=0)
+    gathered = jnp.concatenate(blocks, axis=0)
     half_index = lax.axis_index("cfg")
     conditional = lax.dynamic_index_in_dim(gathered[0], half_index, 1, keepdims=False)
     unconditional = lax.dynamic_index_in_dim(gathered[1], half_index, 1, keepdims=False)

time: 36.6 us -> 38.1 us (1.041)
  starting transfers between devices: 9.62 us -> 13 us
  blocking collectives: 1.9 us -> 0 us
  other arithmetic: 4.12 us -> 4.94 us
  local copies, waits for them, and re-layouts: 9.76 us -> 9.05 us
    all_to_all x0 -> x1, starting transfers between devices: none -> 3.39 us  [per_device(): blocks = lax.all_to_all(blocks, 'cfg', split_axis=0, concat_axis=0)]
    all_gather x1 -> x0, blocking collectives: 1.9 us -> none  [per_device(): gathered = lax.all_gather(local_block[None], 'cfg', axis=0, tiled=True)]
    dynamic_slice x1, local copies, waits for them, and re-layouts: 1.39 us -> 0.65 us  [per_device(): sigma_now = step_table[step_index].astype(jnp.float32) / 1000.0]
    another operation x0 -> x1, other arithmetic: none -> 0.7 us  [per_device(): blocks = jnp.stack([x for _ in range(size)])]
  transfers between devices with their start and end apart: 3 -> 4, of which waited for: 2 -> 2; matrix products, arithmetic and copies ran while one was open for 0% -> 2% of each run, Pallas kernels for 0% -> 0%
where the time goes in v1:
time: 38.1 us; the launch traced here: 37.5 us
  starting transfers between devices  13 us (34%)
  local copies, waits for them, and re-layouts  9.05 us (24%)
  other arithmetic  4.94 us (13%)
  waiting for transfers between devices  4.13 us (11%)
  matrix products  3.56 us (9%)
  between operations  2.85 us (7%)
    ppermute x1, starting transfers between devices, padded_2(): lax.ppermute(lax.slice_in_dim(block, block.shape[dim] - width, None, axis...  4.5 us
    all_to_all x1, starting transfers between devices, per_device(): blocks = lax.all_to_all(blocks, 'cfg', split_axis=0, concat_axis=0)  3.39 us
    ppermute x1, starting transfers between devices, shifted(): return lax.ppermute(block, axis, route)  3.2 us
    ppermute x1, waiting for transfers between devices, padded_2(): lax.ppermute(lax.slice_in_dim(block, 0, width, axis=dim), axis, backward)  3.12 us
    concatenate x1, local copies, waits for them, and re-layouts, conv_taps(): return jnp.concatenate(pieces, axis=-1)  2.88 us
    reduce_sum x1, other arithmetic, head_rows(): center = jnp.mean(values, axis=-1, keepdims=True)  2.21 us
    slice x3, local copies, waits for them, and re-layouts, conv_taps(): padded[step_time:step_time + frames, step_row:step_row + row_count, step_...  2.18 us
    dot_general x1, matrix products, per_device(): jnp.dot(tap_columns, kernel, preferred_element_type=jnp.float32)  2.16 us
  transfers between devices with their start and end apart: 4, of which 2 were waited for; matrix products, arithmetic and copies ran while one was open for 2% of the time, Pallas kernels for 0%

profile of v1, /device:TPU:1, one launch (start us, length us, event | category | flops | bytes accessed | tf_op | source)
XLA Modules:
  0.0 37.5 jit_solution(14054765211921625573)
XLA Ops:
  0.0 1.0 %slice_add_fusion = (f32[1,5120]{1,0:T(1,128)S(1)}, f32[1,5120]{1,0:T(1,128)S(1)}) fusion(f32[2,5120]{1,0:T(2,128)} %param.18), kind=kLoop, calls=%fused_computation.27 | loop fusion | flops 5120 | bytes 81920 | tf_op jit(solution)/shard_map/add | solution.py:35
  1.0 2.2 %convert_reduce_fusion = f32[256]{0:T(256)S(1)} fusion(bf16[1,256,5120]{2,1,0:T(8,128)(2,1)} %param.14), kind=kLoop, calls=%fused_computation.1 | loop fusion | flops 2621184 | bytes 2622464 | tf_op jit(solution)/shard_map/reduce_sum | solution.py:32
  3.2 0.8 %fusion.3 = f32[256]{0:T(256)S(1)} fusion(bf16[1,256,5120]{2,1,0:T(8,128)(2,1)S(1)} %copy-done.1, f32[256]{0:T(256)S(1)} %broadcast_multiply_fusion), kind=kLoop, calls=%fused_computation.6 | loop fusion | flops 5242624 | bytes 2623488 | tf_op jit(solution)/shard_map/reduce_sum | solution.py:33
  4.1 0.0 copy-start.3
  4.2 1.2 %fusion.7 = f32[256,64]{1,0:T(8,128)S(1)} fusion(bf16[5120,64]{0,1:T(8,128)(2,1)S(1)} %copy-done, bf16[1,256,5120]{2,1,0:T(8,128)(2,1)S(1)} %copy-done.1, f32[5120]{0:T(1024)S(1)} %bitcast.57, f32[5120]{0:T(1024)S(1)} %bitcast.56, f32[256]{0:T(256)S(1)} %add_rsqrt_fusion, f32[256]{0:T(256)S(1)} %broadcast_multiply_fusion), kind=kOutput, calls=%fused_computation.10 | convolution fusion | flops 175636480 | bytes 3385344 | tf_op jit(solution)/shard_map/dot_general | solution.py:36
  5.4 1.2 %scatter_custom_fusion = f32[256,64]{1,0:T(8,128)S(1)} fusion(s32[256]{0:T(256)S(1)} %compare_select_fusion, f32[256,64]{1,0:T(8,128)S(1)} %fusion.7, f32[]{:T(128)} %constant.82.clone.1), kind=kCustom, calls=%fused_computation.17 | custom fusion | bytes 65540 | tf_op jit(solution)/shard_map/scatter | solution.py:81
  6.6 0.1 copy.24
  6.6 0.1 reshape.54
  6.8 0.3 copy.25
  7.0 0.7 %stack_broadcast_in_dim_reshape.4 = f32[1,1,2,2,2,2048]{5,4,3,2,1,0:T(2,128)S(1)} reshape(f32[2,2,2,64,2,16]{5,4,3,2,1,0:T(2,128)S(1)} %copy.25) | data formatting | bytes 131072 | tf_op jit(solution)/shard_map/stack;broadcast_in_dim;reshape | solution.py:86
  7.7 0.7 %pad_maximum_fusion = f32[2,1,2,2,2,2048]{5,4,3,2,1,0:T(2,128)} fusion(f32[1,1,2,2,2,2048]{5,4,3,2,1,0:T(2,128)S(1)} %stack_broadcast_in_dim_reshape.4), kind=kLoop, calls=%fused_computation.15 | loop fusion | flops 32768 | bytes 196608 | tf_op jit(solution)/shard_map/stack | solution.py:86
  8.4 3.4 %all-to-all-start = ((f32[2,1,2,2,2,2048]{5,4,3,2,1,0:T(2,128)}), f32[2,1,2,2,2,2048]{5,4,3,2,1,0:T(2,128)S(1)}, u32[]{:S(2)}, u32[]{:S(2)}) async-start(f32[2,1,2,2,2,2048]{5,4,3,2,1,0:T(2,128)} %pad_maximum_fusion), calls=%async_computation | async-start | bytes 262144 | tf_op jit(solution)/shard_map/all_to_all | solution.py:87
  12.5 0.7 %fusion.30 = (s32[1]{0:T(128)}, s32[1]{0:T(128)}) fusion(s32[9]{0:T(128)S(1)} %copy-done.3, s32[]{:T(128)S(6)} %select_n.38, s32[]{:T(128)S(6)} %select_n.37), kind=kLoop, calls=%fused_computation.74 | loop fusion | bytes 24 | tf_op jit(solution)/shard_map/dynamic_slice | solution.py:94
  15.1 0.1 reshape.55
  15.3 0.1 copy.26
  15.4 0.0 copy-done.8
  15.4 0.2 fusion.10
  15.7 0.1 copy.28
  15.8 0.2 reshape.56
  16.0 4.5 %collective-permute-start = (bf16[2,1,2048]{2,1,0:T(2,128)(2,1)S(1)}, bf16[2,1,2048]{2,1,0:T(2,128)(2,1)S(1)}, u32[]{:S(2)}, u32[]{:S(2)}) collective-permute-start(bf16[2,1,2048]{2,1,0:T(2,128)(2,1)S(1)} %get-tuple-element.36), channel_id=1, source_target_pairs={{0,1},{1,2},{2,3},{4,5},{5,6},{6,7},{8,9},{9,10},{10,11},{12,13},{... | collective-permute-start | bytes 24584 | tf_op jit(solution)/shard_map/ppermute | solution.py:16
  20.5 1.9 %collective-permute-start.1 = (bf16[2,1,2048]{2,1,0:T(2,128)(2,1)S(1)}, bf16[2,1,2048]{2,1,0:T(2,128)(2,1)S(1)}, u32[]{:S(2)}, u32[]{:S(2)}) collective-permute-start(bf16[2,1,2048]{2,1,0:T(2,128)(2,1)S(1)} %get-tuple-element.37), channel_id=1, source_target_pairs={{1,0},{2,1},{3,2},{5,4},{6,5},{7,6},{9,8},{10,9},{11,10},{13,12},{... | collective-permute-start | bytes 24584 | tf_op jit(solution)/shard_map/ppermute | solution.py:19
  22.4 3.1 %collective-permute-done.1 = bf16[2,1,2048]{2,1,0:T(2,128)(2,1)S(1)} collective-permute-done((bf16[2,1,2048]{2,1,0:T(2,128)(2,1)S(1)}, bf16[2,1,2048]{2,1,0:T(2,128)(2,1)S(1)}, u32[]{:S(2)}, u32[]{:S(2)}) %collective-permute-start.1) | collective-permute-done | bytes 8224 | tf_op jit(solution)/shard_map/ppermute | solution.py:19
  25.6 0.1 pad_maximum_fusion.1
  25.6 3.2 %collective-permute-start.2 = (bf16[2,4,2048]{2,1,0:T(4,128)(2,1)S(1)}, bf16[2,4,2048]{2,1,0:T(4,128)(2,1)S(1)}, u32[]{:S(2)}, u32[]{:S(2)}) collective-permute-start(bf16[2,4,2048]{2,1,0:T(4,128)(2,1)S(1)} %pad_maximum_fusion.1), channel_id=1, source_target_pairs={{0,4},{4,8},{8,12},{1,5},{5,9},{9,13},{2,6},{6,10},{10,14},{3,7},{... | collective-permute-start | bytes 98312 | tf_op jit(solution)/shard_map/ppermute | solution.py:27
  28.8 1.0 %collective-permute-done.2 = bf16[2,4,2048]{2,1,0:T(4,128)(2,1)S(1)} collective-permute-done((bf16[2,4,2048]{2,1,0:T(4,128)(2,1)S(1)}, bf16[2,4,2048]{2,1,0:T(4,128)(2,1)S(1)}, u32[]{:S(2)}, u32[]{:S(2)}) %collective-permute-start.2) | collective-permute-done | bytes 32800 | tf_op jit(solution)/shard_map/ppermute | solution.py:27
  29.8 0.1 maximum_maximum_fusion
  29.9 0.4 reshape.57
  30.3 0.3 pad_slice_fusion.1
  30.6 1.0 %pad_slice_fusion = (bf16[2,2,128,16]{3,2,1,0:T(8,128)(2,1)S(1)}, bf16[2,2,128,16]{3,2,1,0:T(8,128)(2,1)S(1)}, bf16[2,2,128,16]{3,2,1,0:T(8,128)(2,1)S(1)}, bf16...) fusion(bf16[4,4,128,16]{3,2,1,0:T(8,128)(2,1)S(1)} %reshape.57), kind=kLoop, calls=%fused_computation.53 | loop fusion | bytes 819200 | tf_op jit(solution)/shard_map/slice | solution.py:45
  31.6 0.9 %fusion.27 = (bf16[2,2,128,16]{3,2,1,0:T(8,128)(2,1)}, bf16[2,2,128,16]{3,2,1,0:T(8,128)(2,1)}, bf16[2,2,128,16]{3,2,1,0:T(8,128)(2,1)}, bf16[2,2,128,16]{3,2,1,...) fusion(bf16[4,4,128,16]{3,2,1,0:T(8,128)(2,1)S(1)} %reshape.57), kind=kLoop, calls=%fused_computation.71 | loop fusion | bytes 1277952 | tf_op jit(solution)/shard_map/slice | solution.py:45
  32.5 2.9 %concatenate.11 = bf16[2,2,128,432]{3,2,1,0:T(8,128)(2,1)S(1)} concatenate(bf16[2,2,128,16]{3,2,1,0:T(8,128)(2,1)} %get-tuple-element.31, bf16[2,2,128,16]{3,2,1,0:T(8,128)(2,1)} %get-tuple-element.30, bf16[2,2,128,16]{3,2,1,0:T(8,128)(2,1)S(1)} %get-tuple-element.6, bf16[2,2,128,16]{3,2,1,0:T(8,128)(2,1)S(1)} %get-tuple-element.7, bf16[2,2,128,16]{3,2,1,0:T(8,128)(2,1)} %get-tuple-element.29, ...), dimensions={3} | concatenate | bytes 884736 | tf_op jit(solution)/shard_map/concatenate | solution.py:52
  35.4 2.2 %fusion.9 = bf16[512,384]{1,0:T(8,128)(2,1)} fusion(bf16[512,432]{1,0:T(8,128)(2,1)S(1)} %bitcast.55, bf16[432,384]{1,0:T(8,128)(2,1)} %bitcast.58, f32[384]{0:T(512)S(1)} %copy-done.6), kind=kOutput, calls=%fused_computation.12 | convolution fusion | flops 170262528 | bytes 1168896 | tf_op jit(solution)/shard_map/dot_general | solution.py:113
  (26 shorter events, 0.2 us)
Async XLA Ops:
  0.0 4.1 %copy-start = (bf16[5120,64]{0,1:T(8,128)(2,1)S(1)}, bf16[5120,64]{0,1:T(8,128)(2,1)}, u32[]{:S(2)}) copy-start(bf16[5120,64]{0,1:T(8,128)(2,1)} %param.17) | copy-start | bytes 1966084
  0.0 3.2 %copy-start.1 = (bf16[1,256,5120]{2,1,0:T(8,128)(2,1)S(1)}, bf16[1,256,5120]{2,1,0:T(8,128)(2,1)}, u32[]{:S(2)}) copy-start(bf16[1,256,5120]{2,1,0:T(8,128)(2,1)} %param.14) | copy-start | bytes 7864324
  1.0 3.1 %copy-start.4 = (s32[256]{0:T(256)S(1)}, s32[256]{0:T(256)}, u32[]{:S(2)}) copy-start(s32[256]{0:T(256)} %param.15) | copy-start | bytes 3076
  4.1 8.4 %copy-start.3 = (s32[9]{0:T(128)S(1)}, s32[9]{0:T(128)}, u32[]{:S(2)}) copy-start(s32[9]{0:T(128)} %param.21) | copy-start | bytes 112
  4.1 10.9 %copy-start.2 = (f32[2,2,2048]{2,1,0:T(2,128)S(1)}, f32[2,2,2048]{2,1,0:T(2,128)}, u32[]{:S(2)}) copy-start(f32[2,2,2048]{2,1,0:T(2,128)} %param.16) | copy-start | bytes 98308
  5.3 10.1 %copy-start.5 = (f32[16,16]{1,0:T(8,128)S(1)}, f32[16,16]{1,0:T(8,128)}, u32[]{:S(2)}) copy-start(f32[16,16]{1,0:T(8,128)} %param.24) | copy-start | bytes 3076
  5.3 10.1 %copy-start.7 = (f32[16]{0:T(128)S(1)}, f32[16]{0:T(128)}, u32[]{:S(2)}) copy-start(f32[16]{0:T(128)} %param.25) | copy-start | bytes 196
  5.3 10.1 %copy-start.8 = (f32[16]{0:T(128)S(1)}, f32[16]{0:T(128)}, u32[]{:S(2)}) copy-start(f32[16]{0:T(128)} %param.22) | copy-start | bytes 196
  5.3 10.1 %copy-start.9 = (f32[16]{0:T(128)S(1)}, f32[16]{0:T(128)}, u32[]{:S(2)}) copy-start(f32[16]{0:T(128)} %param.23) | copy-start | bytes 196
  8.4 6.6 %all-to-all-start = ((f32[2,1,2,2,2,2048]{5,4,3,2,1,0:T(2,128)}), f32[2,1,2,2,2,2048]{5,4,3,2,1,0:T(2,128)S(1)}, u32[]{:S(2)}, u32[]{:S(2)}) async-start(f32[2,1,2,2,2,2048]{5,4,3,2,1,0:T(2,128)} %pad_maximum_fusion), calls=%async_computation | async-start | bytes 262144 | tf_op jit(solution)/shard_map/all_to_all | solution.py:87
  16.0 6.4 %collective-permute-start = (bf16[2,1,2048]{2,1,0:T(2,128)(2,1)S(1)}, bf16[2,1,2048]{2,1,0:T(2,128)(2,1)S(1)}, u32[]{:S(2)}, u32[]{:S(2)}) collective-permute-start(bf16[2,1,2048]{2,1,0:T(2,128)(2,1)S(1)} %get-tuple-element.36), channel_id=1, source_target_pairs={{0,1},{1,2},{2,3},{4,5},{5,6},{6,7},{8,9},{9,10},{10,11},{12,13},{... | collective-permute-start | bytes 24584 | tf_op jit(solution)/shard_map/ppermute | solution.py:16
  20.5 5.1 %collective-permute-start.1 = (bf16[2,1,2048]{2,1,0:T(2,128)(2,1)S(1)}, bf16[2,1,2048]{2,1,0:T(2,128)(2,1)S(1)}, u32[]{:S(2)}, u32[]{:S(2)}) collective-permute-start(bf16[2,1,2048]{2,1,0:T(2,128)(2,1)S(1)} %get-tuple-element.37), channel_id=1, source_target_pairs={{1,0},{2,1},{3,2},{5,4},{6,5},{7,6},{9,8},{10,9},{11,10},{13,12},{... | collective-permute-start | bytes 24584 | tf_op jit(solution)/shard_map/ppermute | solution.py:19
  25.6 4.2 %collective-permute-start.2 = (bf16[2,4,2048]{2,1,0:T(4,128)(2,1)S(1)}, bf16[2,4,2048]{2,1,0:T(4,128)(2,1)S(1)}, u32[]{:S(2)}, u32[]{:S(2)}) collective-permute-start(bf16[2,4,2048]{2,1,0:T(4,128)(2,1)S(1)} %pad_maximum_fusion.1), channel_id=1, source_target_pairs={{0,4},{4,8},{8,12},{1,5},{5,9},{9,13},{2,6},{6,10},{10,14},{3,7},{... | collective-permute-start | bytes 98312 | tf_op jit(solution)/shard_map/ppermute | solution.py:27
  31.6 3.8 %copy-start.6 = (f32[384]{0:T(512)S(1)}, f32[384]{0:T(512)}, u32[]{:S(2)}) copy-start(f32[384]{0:T(512)} %param.27) | copy-start | bytes 4612
